TPU v7x, 512 devices: a whole 4x4x16 slice. The times are simulated.
512 devices in a mesh: row: 16 (over x, y), col: 32 (over z, core).
Axes of the slice: x: 4, y: 4, z: 16, core: 2. Of those that a mesh axis runs over, the one named last changes fastest.
Arguments:
- rhs: float32 [36864, 128], P('row'), may hold values from -6 to 6
- factor: float32 [34816, 4096], P('row', 'col'), may hold values from -0.09375 to 0.09375
- inverses: float32 [2, 2048, 2048], P(None, 'col', 'row'), may hold values from -1 to 3, as said below
Outputs:
- solution: float32 [4096, 128], P('col')
- remaining: float32 [32768, 128], P('row')
Inputs may be any that keep to these rules, and one draw needn't show every extreme that they name: Each inverses[k] is lower triangular in panel order with positive diagonal entries.
All inputs are finite; a program needn't handle non-finite values.
Results may differ from a plain program's by a relative error of at most 0.000068.
Values sent between devices are 32-bit elements; how exact they have to be, the bound alone decides.
No kernel may reach another device: no remote copies, remote signals or barrier semaphores. Data moves between devices by JAX's collectives and lax.ppermute only.
A program may use at most 64 MiB of HBM per device.

v0:
```python
import jax
import jax.numpy as jnp
from jax import lax
from jax.experimental.layout import Layout, with_layout_constraint
from jax.sharding import Mesh
from jax.sharding import PartitionSpec as P

ROW = ("x", "y")
NEAR = ("pair", "core")
Z = ("parity", "pair")
COL = (*Z, "core")
SWAP = [(0, 1), (1, 0)]


def exchanged(blocks, axis):
    return lax.all_to_all(blocks, axis, split_axis=0, concat_axis=0, tiled=True)


def from_everyone(array, axis):
    return exchanged(jnp.broadcast_to(array, (lax.axis_size(axis), *array.shape)), axis)


def taken_together(array, axis):
    return jnp.sum(from_everyone(array, axis), axis=0)


def my_sum(array, axis):
    count = lax.axis_size(axis)
    blocks = array.reshape(count, array.shape[0] // count, *array.shape[1:])
    return jnp.sum(exchanged(blocks, axis), axis=0)


def product(left, right, precision=lax.Precision.HIGHEST):
    return jnp.dot(left, right, precision=precision, preferred_element_type=jnp.float32)


def part_of(array, start, rows):
    return lax.dynamic_slice(
        array, (start, 0), (rows, array.shape[1]), allow_negative_indices=False
    )


def quarter_of(blocks, first, pair):
    sizes = (blocks.shape[0] // 2, 1, *blocks.shape[2:])
    part = lax.dynamic_slice(blocks, (first, pair, 0, 0), sizes, allow_negative_indices=False)
    return part.reshape(-1, blocks.shape[-1])


def local(rhs, factor, inverses):
    span_rows = inverses.shape[2]
    span_cols = factor.shape[1] // 2
    first_rhs = rhs[:span_rows]
    second_rhs = rhs[span_rows : 2 * span_rows]
    spots = lax.axis_size(Z)
    rows = (rhs.shape[0] - 2 * span_rows) // (2 * spots)
    half = spots * rows
    side = lax.axis_index("core") ^ lax.axis_index("pair")
    pair = lax.axis_index("pair")
    place = 2 * span_rows + side * half + lax.axis_index(Z) * rows
    near_rows = span_rows // lax.axis_size(NEAR)
    near = lax.axis_index(NEAR) * near_rows
    core, other_core = (lax.axis_index("core"), 1 - lax.axis_index("core"))
    other_pair, group = (1 - pair, spots // 2)
    unknowns = factor.shape[1]
    starts = (
        1 + side * group,
        1 + (1 - side) * group,
        pair,
        other_pair,
        near,
        place,
        (pair * 2 + other_core) * unknowns,
        (other_pair * 2 + other_core) * unknowns,
        (other_pair * 2 + core) * unknowns,
    )
    first_part = product(inverses[0], first_rhs)
    first_part, second_rhs, starts = lax.optimization_barrier((first_part, second_rhs, starts))
    blocks_at, other_at, pair, other_pair, near, place, across_at, crossed_at, straight_at = starts
    first_sol = taken_together(first_part, ROW)
    coupled = lax.optimization_barrier(product(factor[:span_rows, :span_cols], first_sol))
    coupled = with_layout_constraint(coupled, Layout((0, 1)))
    coupled = lax.all_gather(coupled, NEAR, axis=0)
    coupled = lax.dynamic_slice(
        coupled,
        (0, near, 0),
        (coupled.shape[0], near_rows, coupled.shape[2]),
        allow_negative_indices=False,
    )
    coupled = jnp.sum(coupled, axis=0)
    coupled = lax.all_gather(taken_together(coupled, "parity"), NEAR, axis=0, tiled=True)
    second_part = product(inverses[1], second_rhs - coupled)
    second_part, factor, rhs = lax.optimization_barrier((second_part, factor, rhs))
    blocks = factor.reshape(-1, 2, rows, factor.shape[1])
    own = quarter_of(blocks, blocks_at, pair)
    across = quarter_of(blocks, other_at, pair)
    crossed = quarter_of(blocks, blocks_at, other_pair)
    straight = quarter_of(blocks, other_at, other_pair)
    across = lax.ppermute(across, NEAR, [(0, 1), (1, 0), (2, 3), (3, 2)])
    crossed = lax.ppermute(crossed, NEAR, [(0, 3), (3, 0), (1, 2), (2, 1)])
    straight = lax.ppermute(straight, NEAR, [(0, 2), (2, 0), (1, 3), (3, 1)])
    trailing = part_of(rhs, place, rows)
    second_sol = taken_together(second_part, ROW)
    second_sol, own, trailing = lax.optimization_barrier((second_sol, own, trailing))
    both = lax.optimization_barrier(jnp.concatenate([first_sol, second_sol], 0))
    near_both = lax.all_gather(both, NEAR, axis=0, tiled=True)
    theirs = [part_of(near_both, at, both.shape[0]) for at in (across_at, crossed_at, straight_at)]
    columns = jnp.concatenate([own, across, crossed, straight], 1)
    terms = product(columns, jnp.concatenate([both, *theirs], 0), lax.Precision.HIGH)
    terms = my_sum(with_layout_constraint(terms, Layout((0, 1))), "parity")
    rings = [[2 * z + (z + start) % 2 for z in range(spots)] for start in range(2)]
    mine = lax.all_gather(trailing - terms, COL, axis=0, tiled=True, axis_index_groups=rings)
    other = lax.ppermute(mine, "core", SWAP)
    remaining = jnp.where(
        side == 0, jnp.concatenate([mine, other], 0), jnp.concatenate([other, mine], 0)
    )
    return (both, remaining)


def solution(mesh):
    rows, cols = mesh.devices.shape
    shape = (4, rows // 4, cols // 4, 2, 2)
    torus = Mesh(mesh.devices.reshape(shape), (*ROW, *COL))
    in_specs = (P(ROW, None), P(ROW, COL), P(None, COL, ROW))
    out_specs = (P(COL, None), P(ROW, None))
    return jax.shard_map(local, mesh=torus, in_specs=in_specs, out_specs=out_specs, check_vma=False)
```

profile of v0, /device:TPU:1, one launch (start us, length us, event | category | flops | bytes accessed | tf_op | source)
XLA Modules:
  0.0 142.8 jit_solution(4184857471511900030)
XLA Ops:
  0.7 0.0 copy-start
  0.7 1.1 fusion.17
  1.9 0.0 slice-start
  1.9 0.0 copy-start.3
  1.9 16.7 %all_to_all.20 = f32[16,64,128]{2,1,0:T(8,128)S(1)} all-to-all(f32[16,64,128]{2,1,0:T(8,128)S(1)} %broadcast_in_dim.9), channel_id=1, replica_groups=mesh['x'=4,'y'=4,'parity'=8,'pair'=2,'core'=2] {'x','y'}, dimensions={0} | all-to-all | bytes 1048576 | tf_op jit(solution)/shard_map/all_to_all | solution.py:16
  18.6 0.0 copy-done
  18.7 0.2 convolution_bitcast_fusion
  18.9 9.2 %all-gather = f32[512,128]{1,0:T(8,128)S(1)} all-gather(f32[128,128]{1,0:T(8,128)S(1)} %convolution_bitcast_fusion), channel_id=2, replica_groups=mesh['x'=4,'y'=4,'parity'=8,'pair'=2,'core'=2] {'pair','core'}, dimensions={0}, use_global_device_ids=true | all-gather | bytes 327680 | tf_op jit(solution)/shard_map/all_gather | solution.py:82
  28.1 27.8 %all_to_all.21 = f32[8,32,128]{2,1,0:T(8,128)S(1)} all-to-all(f32[8,32,128]{2,1,0:T(8,128)S(1)} %broadcast_in_dim.10), channel_id=1, replica_groups=mesh['x'=4,'y'=4,'parity'=8,'pair'=2,'core'=2] {'parity'}, dimensions={0} | all-to-all | bytes 262144 | tf_op jit(solution)/shard_map/all_to_all | solution.py:16
  55.9 8.4 %all_gather.17 = f32[128,128]{1,0:T(8,128)S(1)} all-gather(f32[32,128]{1,0:T(8,128)S(1)} %reduce_sum.47), channel_id=1, replica_groups=mesh['x'=4,'y'=4,'parity'=8,'pair'=2,'core'=2] {'pair','core'}, dimensions={0}, use_global_device_ids=true | all-gather | bytes 81920 | tf_op jit(solution)/shard_map/all_gather | solution.py:90
  64.4 0.0 slice-done
  64.4 0.0 copy-done.3
  64.4 0.2 convolution_bitcast_fusion.1
  64.6 0.8 broadcast_in_dim.11
  65.4 3.6 %all-to-all-start.2 = ((f32[16,64,128]{2,1,0:T(8,128)}), f32[16,64,128]{2,1,0:T(8,128)S(1)}, u32[]{:S(2)}, u32[]{:S(2)}) async-start(f32[16,64,128]{2,1,0:T(8,128)} %broadcast_in_dim.11), calls=%async_computation.2 | async-start | bytes 1048576 | tf_op jit(solution)/shard_map/all_to_all | solution.py:16
  69.0 0.0 copy-start.2
  69.0 0.1 constant_dynamic-slice_fusion.5
  69.1 2.4 %collective-permute-start.2 = (f32[512,128]{1,0:T(8,128)S(1)}, f32[512,128]{1,0:T(8,128)S(1)}, u32[]{:S(2)}, u32[]{:S(2)}) collective-permute-start(f32[512,128]{1,0:T(8,128)S(1)} %bitcast.23), channel_id=1, source_target_pairs={{0,2},{2,0},{1,3},{3,1},{4,6},{6,4},{5,7},{7,5},{8,10},{10,8},{9,1... | collective-permute-start | bytes 786440 | tf_op jit(solution)/shard_map/ppermute | solution.py:100
  71.6 2.4 %collective-permute-start = (f32[512,128]{1,0:T(8,128)S(1)}, f32[512,128]{1,0:T(8,128)S(1)}, u32[]{:S(2)}, u32[]{:S(2)}) collective-permute-start(f32[512,128]{1,0:T(8,128)S(1)} %bitcast.22), channel_id=1, source_target_pairs={{0,1},{1,0},{2,3},{3,2},{4,5},{5,4},{6,7},{7,6},{8,9},{9,8},{10,11... | collective-permute-start | bytes 786440 | tf_op jit(solution)/shard_map/ppermute | solution.py:98
  73.9 3.0 %collective-permute-start.1 = (f32[512,128]{1,0:T(8,128)S(1)}, f32[512,128]{1,0:T(8,128)S(1)}, u32[]{:S(2)}, u32[]{:S(2)}) collective-permute-start(f32[512,128]{1,0:T(8,128)S(1)} %bitcast.21), channel_id=1, source_target_pairs={{0,3},{3,0},{1,2},{2,1},{4,7},{7,4},{5,6},{6,5},{8,11},{11,8},{9,1... | collective-permute-start | bytes 786440 | tf_op jit(solution)/shard_map/ppermute | solution.py:99
  76.9 0.0 copy-done.2
  76.9 2.6 %all-to-all-done.2 = f32[16,64,128]{2,1,0:T(8,128)S(1)} async-done(((f32[16,64,128]{2,1,0:T(8,128)}), f32[16,64,128]{2,1,0:T(8,128)S(1)}, u32[]{:S(2)}, u32[]{:S(2)}) %all-to-all-start.2) | async-done | bytes 524320 | tf_op jit(solution)/shard_map/all_to_all | solution.py:16
  79.5 0.0 copy-start.1
  79.5 8.0 %all_gather.18 = f32[512,128]{1,0:T(8,128)S(1)} all-gather(f32[128,128]{1,0:T(8,128)S(1)} %pad_maximum_fusion), channel_id=1, replica_groups=mesh['x'=4,'y'=4,'parity'=8,'pair'=2,'core'=2] {'pair','core'}, dimensions={0}, use_global_device_ids=true | all-gather | bytes 327680 | tf_op jit(solution)/shard_map/all_gather | solution.py:105
  87.6 0.0 collective-permute-done.2
  87.6 0.0 collective-permute-done
  87.6 0.0 collective-permute-done.1
  87.6 0.6 fusion
  88.2 0.0 copy-done.1
  88.3 23.8 %all_to_all.22 = f32[8,64,128]{2,1,0:T(8,128)S(1)} all-to-all(f32[8,64,128]{2,1,0:T(8,128)S(1)} %bitcast.24), channel_id=1, replica_groups=mesh['x'=4,'y'=4,'parity'=8,'pair'=2,'core'=2] {'parity'}, dimensions={0} | all-to-all | bytes 524288 | tf_op jit(solution)/shard_map/all_to_all | solution.py:16
  112.1 25.8 %all_gather.19 = f32[1024,128]{1,0:T(8,128)S(1)} all-gather(f32[64,128]{1,0:T(8,128)S(1)} %sub.19), channel_id=1, replica_groups={{0,3,4,7,8,11,12,15,16,19,20,23,24,27,28,31},{1,2,5,6,9,10,13,14,17,18,..., dimensions={0}, use_global_device_ids=true | all-gather | bytes 557056 | tf_op jit(solution)/shard_map/all_gather | solution.py:111
  137.9 2.2 %collective-permute-start.3 = (f32[1024,128]{1,0:T(8,128)S(1)}, f32[1024,128]{1,0:T(8,128)S(1)}, u32[]{:S(2)}, u32[]{:S(2)}) collective-permute-start(f32[1024,128]{1,0:T(8,128)S(1)} %all_gather.19), channel_id=1, source_target_pairs={{0,1},{1,0},{2,3},{3,2},{4,5},{5,4},{6,7},{7,6},{8,9},{9,8},{10,11... | collective-permute-start | bytes 1572872 | tf_op jit(solution)/shard_map/ppermute | solution.py:112
  140.1 1.6 %collective-permute-done.3 = f32[1024,128]{1,0:T(8,128)S(1)} collective-permute-done((f32[1024,128]{1,0:T(8,128)S(1)}, f32[1024,128]{1,0:T(8,128)S(1)}, u32[]{:S(2)}, u32[]{:S(2)}) %collective-permute-start.3) | collective-permute-done | bytes 524320 | tf_op jit(solution)/shard_map/ppermute | solution.py:112
  141.7 1.1 maximum_select_fusion
  (11 shorter events, 0.2 us)
Async XLA Ops:
  0.7 18.0 %copy-start = (f32[2176,128]{1,0:T(8,128)S(1)}, f32[2176,128]{1,0:T(8,128)}, u32[]{:S(2)}) copy-start(f32[2176,128]{1,0:T(8,128)} %param.4) | copy-start | bytes 3342340
  1.9 62.5 %slice-start = ((f32[2304,128]{1,0:T(8,128)}), f32[128,128]{1,0:T(8,128)S(1)}, s32[]{:S(2)}) async-start(f32[2304,128]{1,0:T(8,128)} %param.3), calls=%async_computation.4 | async-start | bytes 131072 | tf_op jit(solution)/shard_map/slice | solution.py:53
  1.9 62.5 %copy-start.3 = (f32[2,64,128]{2,1,0:T(8,128)S(1)}, f32[2,64,128]{2,1,0:T(8,128)}, u32[]{:S(2)}) copy-start(f32[2,64,128]{2,1,0:T(8,128)} %param.5) | copy-start | bytes 196612
  65.4 14.1 %all-to-all-start.2 = ((f32[16,64,128]{2,1,0:T(8,128)}), f32[16,64,128]{2,1,0:T(8,128)S(1)}, u32[]{:S(2)}, u32[]{:S(2)}) async-start(f32[16,64,128]{2,1,0:T(8,128)} %broadcast_in_dim.11), calls=%async_computation.2 | async-start | bytes 1048576 | tf_op jit(solution)/shard_map/all_to_all | solution.py:16
  69.0 7.9 %copy-start.2 = (f32[2304,128]{1,0:T(8,128)S(1)}, f32[2304,128]{1,0:T(8,128)}, u32[]{:S(2)}) copy-start(f32[2304,128]{1,0:T(8,128)} %param.3) | copy-start | bytes 3538948
  69.1 18.5 %collective-permute-start.2 = (f32[512,128]{1,0:T(8,128)S(1)}, f32[512,128]{1,0:T(8,128)S(1)}, u32[]{:S(2)}, u32[]{:S(2)}) collective-permute-start(f32[512,128]{1,0:T(8,128)S(1)} %bitcast.23), channel_id=1, source_target_pairs={{0,2},{2,0},{1,3},{3,1},{4,6},{6,4},{5,7},{7,5},{8,10},{10,8},{9,1... | collective-permute-start | bytes 786440 | tf_op jit(solution)/shard_map/ppermute | solution.py:100
  71.6 16.1 %collective-permute-start = (f32[512,128]{1,0:T(8,128)S(1)}, f32[512,128]{1,0:T(8,128)S(1)}, u32[]{:S(2)}, u32[]{:S(2)}) collective-permute-start(f32[512,128]{1,0:T(8,128)S(1)} %bitcast.22), channel_id=1, source_target_pairs={{0,1},{1,0},{2,3},{3,2},{4,5},{5,4},{6,7},{7,6},{8,9},{9,8},{10,11... | collective-permute-start | bytes 786440 | tf_op jit(solution)/shard_map/ppermute | solution.py:98
  73.9 13.7 %collective-permute-start.1 = (f32[512,128]{1,0:T(8,128)S(1)}, f32[512,128]{1,0:T(8,128)S(1)}, u32[]{:S(2)}, u32[]{:S(2)}) collective-permute-start(f32[512,128]{1,0:T(8,128)S(1)} %bitcast.21), channel_id=1, source_target_pairs={{0,3},{3,0},{1,2},{2,1},{4,7},{7,4},{5,6},{6,5},{8,11},{11,8},{9,1... | collective-permute-start | bytes 786440 | tf_op jit(solution)/shard_map/ppermute | solution.py:99
  79.5 8.7 %copy-start.1 = (f32[128,128]{1,0:T(8,128)}, f32[128,128]{1,0:T(8,128)S(1)}, u32[]{:S(2)}) copy-start(f32[128,128]{1,0:T(8,128)S(1)} %pad_maximum_fusion) | copy-start | bytes 196612
  137.9 3.8 %collective-permute-start.3 = (f32[1024,128]{1,0:T(8,128)S(1)}, f32[1024,128]{1,0:T(8,128)S(1)}, u32[]{:S(2)}, u32[]{:S(2)}) collective-permute-start(f32[1024,128]{1,0:T(8,128)S(1)} %all_gather.19), channel_id=1, source_target_pairs={{0,1},{1,0},{2,3},{3,2},{4,5},{5,4},{6,7},{7,6},{8,9},{9,8},{10,11... | collective-permute-start | bytes 1572872 | tf_op jit(solution)/shard_map/ppermute | solution.py:112
where the time goes:
time: 143 us
  blocking collectives  120 us (84%)
  starting transfers between devices  13.5 us (9%)
  waiting for transfers between devices  4.16 us (3%)
  matrix products  2.11 us (1%)
    all_to_all x3, blocking collectives, exchanged(): return lax.all_to_all(blocks, axis, split_axis=0, concat_axis=0, tiled=True)  68.3 us
    all_gather x1, blocking collectives, local(): lax.all_gather(trailing - terms, COL, axis=0, tiled=True, axis_index_grou...  25.8 us
    all_gather x1, blocking collectives, local(): coupled = lax.all_gather(coupled, NEAR, axis=0)  9.24 us
    all_gather x1, blocking collectives, local(): lax.all_gather(taken_together(coupled, 'parity'), NEAR, axis=0, tiled=True)  8.44 us
    all_gather x1, blocking collectives, local(): near_both = lax.all_gather(both, NEAR, axis=0, tiled=True)  8.04 us
    all_to_all x1, starting transfers between devices, exchanged(): return lax.all_to_all(blocks, axis, split_axis=0, concat_axis=0, tiled=True)  3.57 us
    ppermute x1, starting transfers between devices, local(): crossed = lax.ppermute(crossed, NEAR, [(0, 3), (3, 0), (1, 2), (2, 1)])  2.95 us
  transfers between devices with their start and end apart: 5, of which 2 were waited for; matrix products, arithmetic and copies ran while one was open for 0% of the time, Pallas kernels for 0%

commit v1 on v0

--- a/solution.py
+++ b/solution.py
@@ -102,7 +102,9 @@
     second_sol = taken_together(second_part, ROW)
     second_sol, own, trailing = lax.optimization_barrier((second_sol, own, trailing))
     both = lax.optimization_barrier(jnp.concatenate([first_sol, second_sol], 0))
-    near_both = lax.all_gather(both, NEAR, axis=0, tiled=True)
+    near_both = jnp.concatenate(
+        lax.all_to_all(jnp.stack([both] * lax.axis_size(NEAR)), NEAR, 0, 0), axis=0
+    )
     theirs = [part_of(near_both, at, both.shape[0]) for at in (across_at, crossed_at, straight_at)]
     columns = jnp.concatenate([own, across, crossed, straight], 1)
     terms = product(columns, jnp.concatenate([both, *theirs], 0), lax.Precision.HIGH)

time: 143 us -> 158 us (1.10)
  waiting for transfers between devices: 4.16 us -> 20.6 us
  blocking collectives: 120 us -> 112 us
  starting transfers between devices: 13.5 us -> 19.1 us
    all_gather x1 -> x0, blocking collectives: 8.04 us -> none  [local(): near_both = lax.all_gather(both, NEAR, axis=0, tiled=True)]
    all_to_all x1, waiting for transfers between devices: 2.57 us -> 10.3 us  [exchanged(): return lax.all_to_all(blocks, axis, split_axis=0, concat_axis=0, tiled=True)]
    ppermute x1, waiting for transfers between devices: 0.01 us -> 5.8 us  [local(): crossed = lax.ppermute(crossed, NEAR, [(0, 3), (3, 0), (1, 2), (2, 1)])]
    all_to_all x0 -> x1, starting transfers between devices: none -> 5.3 us  [local(): lax.all_to_all(jnp.stack([both] * lax.axis_size(NEAR)), NEAR, 0, 0)]
    ppermute x1, waiting for transfers between devices: 0.01 us -> 2.96 us  [local(): straight = lax.ppermute(straight, NEAR, [(0, 2), (2, 0), (1, 3), (3, 1)])]
  transfers between devices with their start and end apart: 5 -> 6, of which waited for: 2 -> 4; matrix products, arithmetic and copies ran while one was open for 0% -> 0% of each run, Pallas kernels for 0% -> 0%
where the time goes in v1:
time: 158 us; the launch traced here: 157 us
  blocking collectives  112 us (71%)
  waiting for transfers between devices  20.6 us (13%)
  starting transfers between devices  19.1 us (12%)
  matrix products  2.1 us (1%)
  local copies, waits for them, and re-layouts  1.81 us (1%)
    all_to_all x3, blocking collectives, exchanged(): return lax.all_to_all(blocks, axis, split_axis=0, concat_axis=0, tiled=True)  68.5 us
    all_gather x1, blocking collectives, local(): lax.all_gather(trailing - terms, COL, axis=0, tiled=True, axis_index_grou...  25.4 us
    all_to_all x1, waiting for transfers between devices, exchanged(): return lax.all_to_all(blocks, axis, split_axis=0, concat_axis=0, tiled=True)  10.3 us
    all_gather x1, blocking collectives, local(): coupled = lax.all_gather(coupled, NEAR, axis=0)  9.24 us
    all_gather x1, blocking collectives, local(): lax.all_gather(taken_together(coupled, 'parity'), NEAR, axis=0, tiled=True)  8.44 us
    ppermute x1, waiting for transfers between devices, local(): crossed = lax.ppermute(crossed, NEAR, [(0, 3), (3, 0), (1, 2), (2, 1)])  5.8 us
    all_to_all x1, starting transfers between devices, local(): lax.all_to_all(jnp.stack([both] * lax.axis_size(NEAR)), NEAR, 0, 0)  5.3 us
    all_to_all x1, starting transfers between devices, exchanged(): return lax.all_to_all(blocks, axis, split_axis=0, concat_axis=0, tiled=True)  3.57 us
  transfers between devices with their start and end apart: 6, of which 4 were waited for; matrix products, arithmetic and copies ran while one was open for 0% of the time, Pallas kernels for 0%

profile of v1, /device:TPU:1, one launch (start us, length us, event | category | flops | bytes accessed | tf_op | source)
XLA Modules:
  0.0 157.2 jit_solution(1876692744442292571)
XLA Ops:
  0.7 0.0 copy-start
  0.7 1.1 fusion.17
  1.9 0.0 slice-start
  1.9 0.0 copy-start.3
  1.9 16.7 %all_to_all.25 = f32[16,64,128]{2,1,0:T(8,128)S(1)} all-to-all(f32[16,64,128]{2,1,0:T(8,128)S(1)} %broadcast_in_dim.9), channel_id=1, replica_groups=mesh['x'=4,'y'=4,'parity'=8,'pair'=2,'core'=2] {'x','y'}, dimensions={0} | all-to-all | bytes 1048576 | tf_op jit(solution)/shard_map/all_to_all | solution.py:16
  18.6 0.0 copy-done
  18.7 0.2 convolution_bitcast_fusion
  18.9 9.2 %all-gather = f32[512,128]{1,0:T(8,128)S(1)} all-gather(f32[128,128]{1,0:T(8,128)S(1)} %convolution_bitcast_fusion), channel_id=2, replica_groups=mesh['x'=4,'y'=4,'parity'=8,'pair'=2,'core'=2] {'pair','core'}, dimensions={0}, use_global_device_ids=true | all-gather | bytes 327680 | tf_op jit(solution)/shard_map/all_gather | solution.py:82
  28.1 0.0 copy-start.2
  28.1 27.9 %all_to_all.26 = f32[8,32,128]{2,1,0:T(8,128)S(1)} all-to-all(f32[8,32,128]{2,1,0:T(8,128)S(1)} %broadcast_in_dim.10), channel_id=1, replica_groups=mesh['x'=4,'y'=4,'parity'=8,'pair'=2,'core'=2] {'parity'}, dimensions={0} | all-to-all | bytes 262144 | tf_op jit(solution)/shard_map/all_to_all | solution.py:16
  56.1 8.4 %all_gather.14 = f32[128,128]{1,0:T(8,128)S(1)} all-gather(f32[32,128]{1,0:T(8,128)S(1)} %reduce_sum.47), channel_id=1, replica_groups=mesh['x'=4,'y'=4,'parity'=8,'pair'=2,'core'=2] {'pair','core'}, dimensions={0}, use_global_device_ids=true | all-gather | bytes 81920 | tf_op jit(solution)/shard_map/all_gather | solution.py:90
  64.5 0.0 slice-done
  64.5 0.0 copy-done.3
  64.5 0.2 convolution_bitcast_fusion.1
  64.7 0.8 broadcast_in_dim.11
  65.6 3.6 %all-to-all-start.2 = ((f32[16,64,128]{2,1,0:T(8,128)}), f32[16,64,128]{2,1,0:T(8,128)S(1)}, u32[]{:S(2)}, u32[]{:S(2)}) async-start(f32[16,64,128]{2,1,0:T(8,128)} %broadcast_in_dim.11), calls=%async_computation.2 | async-start | bytes 1048576 | tf_op jit(solution)/shard_map/all_to_all | solution.py:16
  69.2 0.0 copy-done.2
  69.2 0.1 constant_dynamic-slice_fusion.5
  69.3 10.3 %all-to-all-done.2 = f32[16,64,128]{2,1,0:T(8,128)S(1)} async-done(((f32[16,64,128]{2,1,0:T(8,128)}), f32[16,64,128]{2,1,0:T(8,128)S(1)}, u32[]{:S(2)}, u32[]{:S(2)}) %all-to-all-start.2) | async-done | bytes 524320 | tf_op jit(solution)/shard_map/all_to_all | solution.py:16
  79.7 0.0 copy-start.1
  79.7 0.7 stack.2
  80.4 5.3 %all-to-all-start.3 = ((f32[4,128,128]{2,1,0:T(8,128)}), f32[4,128,128]{2,1,0:T(8,128)S(1)}, u32[]{:S(2)}, u32[]{:S(2)}) async-start(f32[4,128,128]{2,1,0:T(8,128)} %stack.2), calls=%async_computation.3 | async-start | bytes 524288 | tf_op jit(solution)/shard_map/all_to_all | solution.py:106
  85.7 3.3 %collective-permute-start.2 = (f32[512,128]{1,0:T(8,128)S(1)}, f32[512,128]{1,0:T(8,128)S(1)}, u32[]{:S(2)}, u32[]{:S(2)}) collective-permute-start(f32[512,128]{1,0:T(8,128)S(1)} %bitcast.25), channel_id=1, source_target_pairs={{0,2},{2,0},{1,3},{3,1},{4,6},{6,4},{5,7},{7,5},{8,10},{10,8},{9,1... | collective-permute-start | bytes 786440 | tf_op jit(solution)/shard_map/ppermute | solution.py:100
  89.0 2.5 %collective-permute-start = (f32[512,128]{1,0:T(8,128)S(1)}, f32[512,128]{1,0:T(8,128)S(1)}, u32[]{:S(2)}, u32[]{:S(2)}) collective-permute-start(f32[512,128]{1,0:T(8,128)S(1)} %bitcast.24), channel_id=1, source_target_pairs={{0,1},{1,0},{2,3},{3,2},{4,5},{5,4},{6,7},{7,6},{8,9},{9,8},{10,11... | collective-permute-start | bytes 786440 | tf_op jit(solution)/shard_map/ppermute | solution.py:98
  91.6 1.9 %collective-permute-start.1 = (f32[512,128]{1,0:T(8,128)S(1)}, f32[512,128]{1,0:T(8,128)S(1)}, u32[]{:S(2)}, u32[]{:S(2)}) collective-permute-start(f32[512,128]{1,0:T(8,128)S(1)} %bitcast.23), channel_id=1, source_target_pairs={{0,3},{3,0},{1,2},{2,1},{4,7},{7,4},{5,6},{6,5},{8,11},{11,8},{9,1... | collective-permute-start | bytes 786440 | tf_op jit(solution)/shard_map/ppermute | solution.py:99
  93.5 0.0 all-to-all-done.3
  93.5 3.0 %collective-permute-done.2 = f32[512,128]{1,0:T(8,128)S(1)} collective-permute-done((f32[512,128]{1,0:T(8,128)S(1)}, f32[512,128]{1,0:T(8,128)S(1)}, u32[]{:S(2)}, u32[]{:S(2)}) %collective-permute-start.2) | collective-permute-done | bytes 262176 | tf_op jit(solution)/shard_map/ppermute | solution.py:100
  96.5 0.0 collective-permute-done
  96.5 5.8 %collective-permute-done.1 = f32[512,128]{1,0:T(8,128)S(1)} collective-permute-done((f32[512,128]{1,0:T(8,128)S(1)}, f32[512,128]{1,0:T(8,128)S(1)}, u32[]{:S(2)}, u32[]{:S(2)}) %collective-permute-start.1) | collective-permute-done | bytes 262176 | tf_op jit(solution)/shard_map/ppermute | solution.py:99
  102.3 0.6 fusion
  102.9 0.0 copy-done.1
  102.9 23.8 %all_to_all.27 = f32[8,64,128]{2,1,0:T(8,128)S(1)} all-to-all(f32[8,64,128]{2,1,0:T(8,128)S(1)} %bitcast.26), channel_id=1, replica_groups=mesh['x'=4,'y'=4,'parity'=8,'pair'=2,'core'=2] {'parity'}, dimensions={0} | all-to-all | bytes 524288 | tf_op jit(solution)/shard_map/all_to_all | solution.py:16
  126.8 25.4 %all_gather.15 = f32[1024,128]{1,0:T(8,128)S(1)} all-gather(f32[64,128]{1,0:T(8,128)S(1)} %sub.19), channel_id=1, replica_groups={{0,3,4,7,8,11,12,15,16,19,20,23,24,27,28,31},{1,2,5,6,9,10,13,14,17,18,..., dimensions={0}, use_global_device_ids=true | all-gather | bytes 557056 | tf_op jit(solution)/shard_map/all_gather | solution.py:113
  152.1 2.5 %collective-permute-start.3 = (f32[1024,128]{1,0:T(8,128)S(1)}, f32[1024,128]{1,0:T(8,128)S(1)}, u32[]{:S(2)}, u32[]{:S(2)}) collective-permute-start(f32[1024,128]{1,0:T(8,128)S(1)} %all_gather.15), channel_id=1, source_target_pairs={{0,1},{1,0},{2,3},{3,2},{4,5},{5,4},{6,7},{7,6},{8,9},{9,8},{10,11... | collective-permute-start | bytes 1572872 | tf_op jit(solution)/shard_map/ppermute | solution.py:114
  154.6 1.5 collective-permute-done.3
  156.1 1.1 maximum_select_fusion
  (11 shorter events, 0.2 us)
Async XLA Ops:
  0.7 18.0 %copy-start = (f32[2176,128]{1,0:T(8,128)S(1)}, f32[2176,128]{1,0:T(8,128)}, u32[]{:S(2)}) copy-start(f32[2176,128]{1,0:T(8,128)} %param.4) | copy-start | bytes 3342340
  1.9 62.7 %slice-start = ((f32[2304,128]{1,0:T(8,128)}), f32[128,128]{1,0:T(8,128)S(1)}, s32[]{:S(2)}) async-start(f32[2304,128]{1,0:T(8,128)} %param.3), calls=%async_computation.5 | async-start | bytes 131072 | tf_op jit(solution)/shard_map/slice | solution.py:53
  1.9 62.7 %copy-start.3 = (f32[2,64,128]{2,1,0:T(8,128)S(1)}, f32[2,64,128]{2,1,0:T(8,128)}, u32[]{:S(2)}) copy-start(f32[2,64,128]{2,1,0:T(8,128)} %param.5) | copy-start | bytes 196612
  28.1 41.0 %copy-start.2 = (f32[2304,128]{1,0:T(8,128)S(1)}, f32[2304,128]{1,0:T(8,128)}, u32[]{:S(2)}) copy-start(f32[2304,128]{1,0:T(8,128)} %param.3) | copy-start | bytes 3538948
  65.6 14.1 %all-to-all-start.2 = ((f32[16,64,128]{2,1,0:T(8,128)}), f32[16,64,128]{2,1,0:T(8,128)S(1)}, u32[]{:S(2)}, u32[]{:S(2)}) async-start(f32[16,64,128]{2,1,0:T(8,128)} %broadcast_in_dim.11), calls=%async_computation.2 | async-start | bytes 1048576 | tf_op jit(solution)/shard_map/all_to_all | solution.py:16
  79.7 23.2 %copy-start.1 = (f32[128,128]{1,0:T(8,128)}, f32[128,128]{1,0:T(8,128)S(1)}, u32[]{:S(2)}) copy-start(f32[128,128]{1,0:T(8,128)S(1)} %pad_maximum_fusion) | copy-start | bytes 196612
  80.4 13.1 %all-to-all-start.3 = ((f32[4,128,128]{2,1,0:T(8,128)}), f32[4,128,128]{2,1,0:T(8,128)S(1)}, u32[]{:S(2)}, u32[]{:S(2)}) async-start(f32[4,128,128]{2,1,0:T(8,128)} %stack.2), calls=%async_computation.3 | async-start | bytes 524288 | tf_op jit(solution)/shard_map/all_to_all | solution.py:106
  85.7 10.8 %collective-permute-start.2 = (f32[512,128]{1,0:T(8,128)S(1)}, f32[512,128]{1,0:T(8,128)S(1)}, u32[]{:S(2)}, u32[]{:S(2)}) collective-permute-start(f32[512,128]{1,0:T(8,128)S(1)} %bitcast.25), channel_id=1, source_target_pairs={{0,2},{2,0},{1,3},{3,1},{4,6},{6,4},{5,7},{7,5},{8,10},{10,8},{9,1... | collective-permute-start | bytes 786440 | tf_op jit(solution)/shard_map/ppermute | solution.py:100
  89.0 7.5 %collective-permute-start = (f32[512,128]{1,0:T(8,128)S(1)}, f32[512,128]{1,0:T(8,128)S(1)}, u32[]{:S(2)}, u32[]{:S(2)}) collective-permute-start(f32[512,128]{1,0:T(8,128)S(1)} %bitcast.24), channel_id=1, source_target_pairs={{0,1},{1,0},{2,3},{3,2},{4,5},{5,4},{6,7},{7,6},{8,9},{9,8},{10,11... | collective-permute-start | bytes 786440 | tf_op jit(solution)/shard_map/ppermute | solution.py:98
  91.6 10.7 %collective-permute-start.1 = (f32[512,128]{1,0:T(8,128)S(1)}, f32[512,128]{1,0:T(8,128)S(1)}, u32[]{:S(2)}, u32[]{:S(2)}) collective-permute-start(f32[512,128]{1,0:T(8,128)S(1)} %bitcast.23), channel_id=1, source_target_pairs={{0,3},{3,0},{1,2},{2,1},{4,7},{7,4},{5,6},{6,5},{8,11},{11,8},{9,1... | collective-permute-start | bytes 786440 | tf_op jit(solution)/shard_map/ppermute | solution.py:99
  152.1 4.0 %collective-permute-start.3 = (f32[1024,128]{1,0:T(8,128)S(1)}, f32[1024,128]{1,0:T(8,128)S(1)}, u32[]{:S(2)}, u32[]{:S(2)}) collective-permute-start(f32[1024,128]{1,0:T(8,128)S(1)} %all_gather.15), channel_id=1, source_target_pairs={{0,1},{1,0},{2,3},{3,2},{4,5},{5,4},{6,7},{7,6},{8,9},{9,8},{10,11... | collective-permute-start | bytes 1572872 | tf_op jit(solution)/shard_map/ppermute | solution.py:114
